TPU v7x, 256 devices: a whole 4x4x8 slice. The times are simulated.
256 devices in a mesh: area: 16 (over x, y), sec: 16 (over z, core).
Axes of the slice: x: 4, y: 4, z: 8, core: 2. Of those that a mesh axis runs over, the one named last changes fastest.
Arguments:
- spikes: int32 [16, 3, 16384], P('area', None, 'sec'), may hold values 0 or 1
- intra_weight: float32 [16, 128, 8, 128, 128], P('area', 'sec'), may hold values from -0.5 to 0.5
- intra_dest: int32 [16, 128, 8], P('area'), may hold values from 0 to 127, all different within a row
- inter_weight: float32 [16, 128, 2, 128, 128], P('area', 'sec'), may hold values from -0.5 to 0.5
- inter_target: int32 [16, 16, 2], P(None, 'sec'), may hold values from 0 to 15, all different within a row
- v_init: float32 [16, 16384], P('area', 'sec'), may hold values from 0 to 1
- leak: float32 [16, 16384], P('area', 'sec'), may hold values from 0.3 to 0.95
Outputs:
- potential: float32 [16, 16384], P('area', 'sec')
Inputs may be any that keep to these rules, and one draw needn't show every extreme that they name: `intra_dest`: the 8 target blocks of a source block are distinct; some blocks receive far more synapse blocks than others. `inter_target`: the 2 target areas of a section are distinct; some areas are targeted far more often than others.
All inputs are finite; a program needn't handle non-finite values. No bound on the sum of `spikes` on one device may be relied on, other than what follows from the above.
Results may differ from a plain program's by a relative error of at most 0.000058.
Values sent between devices are 32-bit elements; how exact they have to be, the bound alone decides.
A program may use at most 64 MiB of HBM per device.

v0:
```python
import jax
import jax.numpy as jnp
from jax import lax
from jax.sharding import PartitionSpec as P


def body(spikes, intra_weight, intra_dest, inter_weight, inter_target, v_init, leak):
    blocks = intra_weight.shape[1]
    width = intra_weight.shape[-1]
    steps = spikes.shape[1]
    columns = steps * width
    later = (steps - 1) * width
    section = lax.axis_index("sec")
    area_here = lax.axis_index("area")
    block_count = intra_dest.shape[1]
    spiking = spikes[0].astype(jnp.float32).reshape(steps, blocks, width)
    previous = spiking[:-1]
    intra_part = jnp.einsum(
        "tkn,kfnm->kftm", spiking, intra_weight[0], precision=lax.Precision.HIGHEST
    )
    fanout = intra_part.shape[1]
    intra_rows = intra_part.reshape(blocks * fanout, columns)
    dest_flat = intra_dest[0].reshape(-1)
    my_dest = lax.dynamic_slice_in_dim(dest_flat, section * blocks * fanout, blocks * fanout, 0)
    picker = (jnp.arange(block_count, dtype=jnp.int32)[:, None] == my_dest[None, :]).astype(
        jnp.float32
    )
    block_grid = jnp.dot(
        picker, intra_rows, precision=lax.Precision.HIGHEST, preferred_element_type=jnp.float32
    )
    intra_current = lax.psum_scatter(block_grid, "sec", scatter_dimension=0, tiled=True)
    inter_part = jnp.einsum(
        "tkn,kjnm->kjtm", previous, inter_weight[0], precision=lax.Precision.HIGHEST
    )
    targets_all = inter_target[:, 0, :]
    fan_areas = targets_all.shape[1]
    picker = (targets_all == area_here).astype(jnp.float32)
    inter_current = jnp.einsum(
        "aj,akjx->kx",
        picker,
        lax.all_gather(inter_part.reshape(1, blocks, fan_areas, later), "area", axis=0, tiled=True),
        precision=lax.Precision.HIGHEST,
    )
    inter_full = jnp.concatenate([jnp.zeros((blocks, width), jnp.float32), inter_current], axis=1)
    current = (intra_current + inter_full).reshape(blocks, steps, width)
    current = current.transpose(1, 0, 2).reshape(steps, blocks * width)
    drive = spikes[0].astype(jnp.float32)
    potential = v_init[0]
    decay = leak[0]
    for moment in range(steps):
        potential = decay * potential * (1.0 - drive[moment]) + current[moment]
    return potential[None]


def solution(mesh):
    in_specs = (
        P("area", None, "sec"),
        P("area", "sec", None, None, None),
        P("area", None, None),
        P("area", "sec", None, None, None),
        P(None, "sec", None),
        P("area", "sec"),
        P("area", "sec"),
    )
    out_specs = P("area", "sec")
    return jax.shard_map(body, mesh=mesh, in_specs=in_specs, out_specs=out_specs, check_vma=False)
```

profile of v0, /device:TPU:1, one launch (start us, length us, event | category | flops | bytes accessed | tf_op | source)
XLA Modules:
  0.0 130.5 jit_solution(11523697200835841770)
XLA Ops:
  6.5 0.0 copy-start
  6.5 0.0 copy-start.4
  6.5 0.0 copy-start.3
  6.5 0.0 copy-start.2
  6.5 0.0 all-reduce.4.cloned.1.call-start
  6.6 0.9 copy.12
  7.5 0.1 reshape_squeeze.3
  7.6 0.7 convert_element_type.11
  8.3 0.1 dynamic_slice.3
  8.4 4.4 %fusion.2 = f32[8,8,3,128]{3,2,1,0:T(4,128)S(1)} fusion(f32[1,8,8,128,128]{4,3,2,1,0:T(8,128)} %param.8, f32[3,8,128,1]{2,1,0,3:T(8,128)S(1)} %bitcast.60), kind=kOutput, calls=%fused_computation.2 | convolution fusion | flops 37748736 | bytes 4304896 | tf_op jit(solution)/shard_map/tkn,kfnm->kftm/dot_general | solution.py:18
  12.8 0.9 fusion.8
  13.7 0.0 all-reduce.4.cloned.1.call-update
  13.8 0.0 copy-done
  13.8 0.7 convolution_bitcast_fusion
  14.5 19.9 %all_gather.3 = f32[16,8,2,256]{3,1,2,0:T(8,128)S(1)} all-gather(f32[1,8,2,256]{3,1,2,0:T(8,128)S(1)} %copy.15), channel_id=1, replica_groups=mesh['area'=16,'sec'=16] {'area'}, dimensions={0}, use_global_device_ids=true | all-gather | bytes 278528 | tf_op jit(solution)/shard_map/all_gather | solution.py:41
  34.4 0.0 copy-done.3
  34.4 0.3 fusion.6
  34.8 0.0 copy-done.4
  34.8 0.6 dynamic-slice
  36.1 86.3 %all-reduce.4.cloned.1.call-done = f32[128,384]{1,0:T(8,128)} async-done(((f32[128,384]{1,0:T(8,128)}), f32[128,384]{1,0:T(8,128)}) %all-reduce.4.cloned.1.call-update) | async-done | bytes 196624
  122.3 0.7 fusion.13
  123.0 0.0 copy-done.2
  123.0 0.0 copy-done.1
  123.0 0.6 fusion.17
  (7 shorter events, 0.0 us)
Async XLA Ops:
  6.5 7.2 %copy-start = (f32[1,8,2,128,128]{4,3,2,1,0:T(8,128)S(1)}, f32[1,8,2,128,128]{4,3,2,1,0:T(8,128)}, u32[]{:S(2)}) copy-start(f32[1,8,2,128,128]{4,3,2,1,0:T(8,128)} %param.10) | copy-start | bytes 3145732
  6.5 28.3 %copy-start.4 = (u32[256]{0:T(256)S(1)}, u32[256]{0:T(256)}, u32[]{:S(2)}) copy-start(u32[256]{0:T(256)} %constant.29) | copy-start | bytes 3076
  6.5 27.9 %copy-start.3 = (s32[16,1,2]{0,2,1:T(2,128)S(1)}, s32[16,1,2]{0,2,1:T(2,128)}, u32[]{:S(2)}) copy-start(s32[16,1,2]{0,2,1:T(2,128)} %param.11) | copy-start | bytes 388
  6.5 116.5 %copy-start.2 = (f32[1,1024]{1,0:T(1,128)S(1)}, f32[1,1024]{1,0:T(1,128)}, u32[]{:S(2)}) copy-start(f32[1,1024]{1,0:T(1,128)} %param.12) | copy-start | bytes 12292
  6.5 116.5 %copy-start.1 = (f32[1,1024]{1,0:T(1,128)S(1)}, f32[1,1024]{1,0:T(1,128)}, u32[]{:S(2)}) copy-start(f32[1,1024]{1,0:T(1,128)} %param.13) | copy-start | bytes 12292
  6.5 115.8 %all-reduce.4.cloned.1.call-start = ((), (), s32[]{:S(2)}) async-start(), calls=%async_computation | async-start | bytes 393216
Sparse Core Ops, SparseCore 0:
  13.9 108.4 all-reduce.3
where the time goes:
time: 131 us
  waiting for transfers between devices  86.3 us (66%)
  blocking collectives  19.9 us (15%)
  between operations  14.2 us (11%)
  matrix products  6.37 us (5%)
  other arithmetic  2.05 us (2%)
  local copies, waits for them, and re-layouts  1.68 us (1%)
    unnamed x2, waiting for transfers between devices  86.3 us
    all_gather x1, blocking collectives, body(): lax.all_gather(inter_part.reshape(1, blocks, fan_areas, later), 'area', a...  19.9 us
    dot_general x1, matrix products, body(): jnp.einsum('tkn,kfnm->kftm', spiking, intra_weight[0], precision=lax.Prec...  4.44 us
  transfers between devices with their start and end apart: 1, of which 1 were waited for; matrix products, arithmetic and copies ran while one was open for 1% of the time, Pallas kernels for 0%

commit v1 on v0

--- a/solution.py
+++ b/solution.py
@@ -2,6 +2,13 @@
 import jax.numpy as jnp
 from jax import lax
 from jax.sharding import PartitionSpec as P
+
+
+def gather_over(x, name, dim):
+    devices = lax.axis_size(name)
+    tiles = jnp.stack([x for _ in range(devices)])
+    tiles = lax.all_to_all(tiles, name, split_axis=0, concat_axis=0)
+    return jnp.concatenate(tiles, axis=dim)
 
 
 def body(spikes, intra_weight, intra_dest, inter_weight, inter_target, v_init, leak):
@@ -38,7 +45,7 @@
     inter_current = jnp.einsum(
         "aj,akjx->kx",
         picker,
-        lax.all_gather(inter_part.reshape(1, blocks, fan_areas, later), "area", axis=0, tiled=True),
+        gather_over(inter_part.reshape(1, blocks, fan_areas, later), "area", 0),
         precision=lax.Precision.HIGHEST,
     )
     inter_full = jnp.concatenate([jnp.zeros((blocks, width), jnp.float32), inter_current], axis=1)

time: 131 us -> 140 us (1.069)
  waiting for transfers between devices: 86.3 us -> 107 us
  blocking collectives: 19.9 us -> 0 us
  starting transfers between devices: 0.04 us -> 7.63 us
    unnamed x2, waiting for transfers between devices: 86.3 us -> 107 us
    all_gather x1 -> x0, blocking collectives: 19.9 us -> none  [body(): lax.all_gather(inter_part.reshape(1, blocks, fan_areas, later), 'area', a...]
    all_to_all x0 -> x1, starting transfers between devices: none -> 7.58 us  [gather_over(): tiles = lax.all_to_all(tiles, name, split_axis=0, concat_axis=0)]
  transfers between devices with their start and end apart: 1 -> 2, of which waited for: 1 -> 1; matrix products, arithmetic and copies ran while one was open for 1% -> 5% of each run, Pallas kernels for 0% -> 0%
where the time goes in v1:
time: 140 us
  waiting for transfers between devices  107 us (76%)
  between operations  14.1 us (10%)
  starting transfers between devices  7.63 us (5%)
  matrix products  6.35 us (5%)
  local copies, waits for them, and re-layouts  2.8 us (2%)
  other arithmetic  2.14 us (2%)
    unnamed x2, waiting for transfers between devices  107 us
    all_to_all x1, starting transfers between devices, gather_over(): tiles = lax.all_to_all(tiles, name, split_axis=0, concat_axis=0)  7.58 us
    dot_general x1, matrix products, body(): jnp.einsum('tkn,kfnm->kftm', spiking, intra_weight[0], precision=lax.Prec...  4.44 us
  transfers between devices with their start and end apart: 2, of which 1 were waited for; matrix products, arithmetic and copies ran while one was open for 5% of the time, Pallas kernels for 0%

profile of v1, /device:TPU:1, one launch (start us, length us, event | category | flops | bytes accessed | tf_op | source)
XLA Modules:
  0.0 139.6 jit_solution(8487511697358232650)
XLA Ops:
  6.5 0.0 copy-start
  6.5 0.0 copy-start.4
  6.5 0.8 convert_element_type.11
  7.4 0.4 copy-done
  7.8 0.7 convolution_bitcast_fusion
  8.5 0.8 stack.3
  9.3 7.6 %all-to-all-start = ((f32[16,1,8,2,256]{4,3,2,1,0:T(2,128)}), f32[16,1,8,2,256]{4,3,2,1,0:T(2,128)S(1)}, u32[]{:S(2)}, u32[]{:S(2)}) async-start(f32[16,1,8,2,256]{4,3,2,1,0:T(2,128)} %stack.3), calls=%async_computation | async-start | bytes 524288 | tf_op jit(solution)/shard_map/all_to_all | solution.py:10
  16.9 0.0 all-reduce.4.cloned.1.call-start
  16.9 0.8 copy.12
  17.7 0.1 reshape_squeeze.3
  17.8 0.1 dynamic_slice.3
  17.9 4.4 %fusion.2 = f32[8,8,3,128]{3,2,1,0:T(4,128)S(1)} fusion(f32[1,8,8,128,128]{4,3,2,1,0:T(8,128)} %param.8, f32[3,8,128,1]{2,1,0,3:T(8,128)S(1)} %bitcast.62), kind=kOutput, calls=%fused_computation.2 | convolution fusion | flops 37748736 | bytes 4304896 | tf_op jit(solution)/shard_map/tkn,kfnm->kftm/dot_general | solution.py:25
  22.3 0.9 fusion.8
  23.2 0.0 all-reduce.4.cloned.1.call-update
  23.3 0.0 copy-done.4
  23.3 0.6 dynamic-slice
  24.5 0.0 copy-done.3
  24.5 0.0 all-to-all-done
  24.5 0.3 fusion.6
  24.9 106.5 %all-reduce.4.cloned.1.call-done = f32[128,384]{1,0:T(8,128)} async-done(((f32[128,384]{1,0:T(8,128)}), f32[128,384]{1,0:T(8,128)}) %all-reduce.4.cloned.1.call-update) | async-done | bytes 196624
  131.4 0.7 fusion.13
  132.1 0.0 copy-done.2
  132.1 0.0 copy-done.1
  132.1 0.6 fusion.17
  (8 shorter events, 0.0 us)
Async XLA Ops:
  6.5 1.2 copy-start
  6.5 16.7 %copy-start.4 = (u32[256]{0:T(256)S(1)}, u32[256]{0:T(256)}, u32[]{:S(2)}) copy-start(u32[256]{0:T(256)} %constant.29) | copy-start | bytes 3076
  6.5 18.0 %copy-start.3 = (s32[16,1,2]{0,2,1:T(2,128)S(1)}, s32[16,1,2]{0,2,1:T(2,128)}, u32[]{:S(2)}) copy-start(s32[16,1,2]{0,2,1:T(2,128)} %param.11) | copy-start | bytes 388
  6.5 125.6 %copy-start.2 = (f32[1,1024]{1,0:T(1,128)S(1)}, f32[1,1024]{1,0:T(1,128)}, u32[]{:S(2)}) copy-start(f32[1,1024]{1,0:T(1,128)} %param.12) | copy-start | bytes 12292
  6.5 125.6 %copy-start.1 = (f32[1,1024]{1,0:T(1,128)S(1)}, f32[1,1024]{1,0:T(1,128)}, u32[]{:S(2)}) copy-start(f32[1,1024]{1,0:T(1,128)} %param.13) | copy-start | bytes 12292
  9.3 15.3 %all-to-all-start = ((f32[16,1,8,2,256]{4,3,2,1,0:T(2,128)}), f32[16,1,8,2,256]{4,3,2,1,0:T(2,128)S(1)}, u32[]{:S(2)}, u32[]{:S(2)}) async-start(f32[16,1,8,2,256]{4,3,2,1,0:T(2,128)} %stack.3), calls=%async_computation | async-start | bytes 524288 | tf_op jit(solution)/shard_map/all_to_all | solution.py:10
  16.9 114.6 %all-reduce.4.cloned.1.call-start = ((), (), s32[]{:S(2)}) async-start(), calls=%async_computation.1 | async-start | bytes 393216
Sparse Core Ops, SparseCore 0:
  23.4 108.0 all-reduce.3
